TPU v7x, 256 devices: a whole 4x4x8 slice. The times are simulated.
256 devices in a mesh: dp: 8 (over y, x_hi), ctx: 32 (over x_lo, z, core).
Axes of the slice: x: 4 (x_hi: 2, x_lo: 2; x = x_hi * 2 + x_lo), y: 4, z: 8, core: 2. Of those that a mesh axis runs over, the one named last changes fastest.
Arguments:
- query_rows: bfloat16 [8, 4096, 2048], P('dp', 'ctx'), may hold values from -6 to 6
- key_rows: bfloat16 [8, 4096, 2048], P('dp', 'ctx'), may hold values from -6 to 6
- value_rows: bfloat16 [8, 4096, 2048], P('dp', 'ctx'), may hold values from -6 to 6
- norm_gain: float32 [2048], replicated, may hold values from 0.1 to 1.9
- out_weight: bfloat16 [2048, 2048], P('ctx'), may hold values from -0.125 to 0.125
- cotangent: bfloat16 [8, 4096, 2048], P('dp', 'ctx'), may hold values from -6 to 6
Outputs:
- mixed: bfloat16 [8, 4096, 2048], P('dp', 'ctx')
- grad_queries: bfloat16 [8, 4096, 2048], P('dp', 'ctx')
- grad_keys: bfloat16 [8, 4096, 2048], P('dp', 'ctx')
- grad_values: bfloat16 [8, 4096, 2048], P('dp', 'ctx')
- grad_weight: float32 [2048, 2048], P('ctx')
All inputs are finite; a program needn't handle non-finite values.
Results may differ from a plain program's by a relative error of at most 0.025.
Values may be sent and summed in bfloat16 or wider, within the bound.
A program may use at most 192 MiB of HBM per device.

v0:
```python
import math
import jax
import jax.numpy as jnp
from jax import lax
from jax.sharding import PartitionSpec as P

HEAD = 128
epsilon = 1e-06
highest_precision = lax.Precision.HIGHEST


def carried_in(value, axis, combine, identity):
    size, index = (lax.axis_size(axis), lax.axis_index(axis))
    everything = lax.all_gather(value, axis)
    start = jnp.broadcast_to(jnp.asarray(identity, value.dtype), value.shape)

    def carried_turn(k, before):
        reached = k < index
        new = combine(before, everything[k])
        return jnp.where(reached, new, before)

    return lax.fori_loop(0, size, carried_turn, start)


def entering(value, axis, combine, identity):
    size, index = (lax.axis_size(axis), lax.axis_index(axis))
    everything = lax.all_gather(value.astype(jnp.bfloat16), axis)
    start = jnp.broadcast_to(jnp.asarray(identity, value.dtype), value.shape)

    def entering_turn(k, before):
        at = size - 1 - k
        reached = at > index
        new = combine(before, everything[at].astype(value.dtype))
        return jnp.where(reached, new, before)

    return lax.fori_loop(0, size, entering_turn, start)


def feature(values):
    wide = values.astype(jnp.float32)
    return jnp.where(wide > 0, wide + 1.0, jnp.exp(jnp.minimum(wide, 0.0))).astype(jnp.bfloat16)


def feature_slope(values):
    wide = values.astype(jnp.float32)
    return jnp.where(wide > 0, 1.0, jnp.exp(jnp.minimum(wide, 0.0)))


def add_states(earlier, later):
    return earlier + later


def on_device(query_rows, key_rows, value_rows, norm_gain, out_weight, cotangent):
    length = query_rows.shape[1]
    width = query_rows.shape[2]
    heads = width // HEAD
    shape3 = (length, heads, HEAD)
    weight = lax.all_gather(out_weight, "ctx", axis=0, tiled=True)
    query_seq = query_rows[0]
    key_seq = key_rows[0]
    query_per_head = feature(query_seq).reshape(shape3)
    key_per_head = feature(key_seq).reshape(shape3)
    value_per_head = value_rows[0].reshape(shape3)
    local_state = jnp.einsum(
        "wmx,wmt->mxt", key_per_head, value_per_head, preferred_element_type=jnp.float32
    )
    zero_state = jnp.zeros_like(local_state)
    prefix_state = carried_in(local_state, "ctx", add_states, zero_state)
    causal = jnp.tril(jnp.ones((length, length), dtype=bool))
    scores = jnp.einsum(
        "thd,shd->hts", query_per_head, key_per_head, preferred_element_type=jnp.float32
    )
    probs = jnp.where(causal, scores, 0.0).astype(jnp.bfloat16)
    query_wide_rows = query_per_head.astype(jnp.float32)
    attended_output = jnp.einsum(
        "hts,shv->thv", probs, value_per_head, preferred_element_type=jnp.float32
    )
    attended_output = attended_output + jnp.einsum(
        "wrf,rfp->wrp", query_wide_rows, prefix_state, precision=highest_precision
    )
    inverse = lax.rsqrt(
        jnp.mean(attended_output * attended_output, axis=-1, keepdims=True) + epsilon
    )
    gain_heads = norm_gain.reshape(heads, HEAD)
    normed = (attended_output * inverse * gain_heads).reshape(length, width).astype(jnp.bfloat16)
    mixed = jnp.dot(normed, weight, preferred_element_type=jnp.float32).astype(jnp.bfloat16)
    upstream = cotangent[0]
    d_normed = lax.dot_general(
        upstream, weight, (((1,), (1,)), ((), ())), preferred_element_type=jnp.float32
    ).reshape(shape3)
    scaled = d_normed * gain_heads
    attended_gradient = (
        inverse
        * (
            scaled
            - attended_output
            * inverse
            * inverse
            * jnp.mean(scaled * attended_output, axis=-1, keepdims=True)
        )
    ).astype(jnp.bfloat16)
    grad_local = jnp.einsum(
        "ibg,ibq->bgq", query_per_head, attended_gradient, preferred_element_type=jnp.float32
    )
    suffix_state = entering(grad_local, "ctx", add_states, zero_state)
    d_scores = jnp.einsum(
        "thv,shv->hts", attended_gradient, value_per_head, preferred_element_type=jnp.float32
    )
    d_probs = jnp.where(causal, d_scores, 0.0).astype(jnp.bfloat16)
    wide_gradient = attended_gradient.astype(jnp.float32)
    value_wide_rows = value_per_head.astype(jnp.float32)
    key_wide_rows = key_per_head.astype(jnp.float32)
    query_gradient = jnp.einsum(
        "hts,shk->thk", d_probs, key_per_head, preferred_element_type=jnp.float32
    )
    query_gradient = query_gradient + jnp.einsum(
        "fxn,xpn->fxp", wide_gradient, prefix_state, precision=highest_precision
    )
    key_gradient = jnp.einsum(
        "hts,thk->shk", d_probs, query_per_head, preferred_element_type=jnp.float32
    )
    key_gradient = key_gradient + jnp.einsum(
        "mcu,cxu->mcx", value_wide_rows, suffix_state, precision=highest_precision
    )
    value_gradient = jnp.einsum(
        "hts,thv->shv", probs, attended_gradient, preferred_element_type=jnp.float32
    )
    value_gradient = value_gradient + jnp.einsum(
        "inz,nzc->inc", key_wide_rows, suffix_state, precision=highest_precision
    )
    grad_queries = (query_gradient.reshape(length, width) * feature_slope(query_seq)).astype(
        jnp.bfloat16
    )
    grad_keys = (key_gradient.reshape(length, width) * feature_slope(key_seq)).astype(jnp.bfloat16)
    grad_values = value_gradient.reshape(length, width).astype(jnp.bfloat16)
    devices_dp = lax.axis_size("dp")
    devices_ctx = lax.axis_size("ctx")
    loss_scale = 1.0 / math.sqrt(devices_dp * devices_ctx * length)
    shares = lax.psum_scatter(
        lax.dot_general(
            normed, upstream, (((0,), (0,)), ((), ())), preferred_element_type=jnp.float32
        ).astype(jnp.bfloat16),
        "ctx",
        scatter_dimension=0,
        tiled=True,
    )
    summed = lax.psum(shares, "dp").astype(jnp.float32)
    grad_weight = summed * loss_scale
    return (mixed[None], grad_queries[None], grad_keys[None], grad_values[None], grad_weight)


def solution(mesh):
    return jax.shard_map(
        on_device,
        mesh=mesh,
        in_specs=(
            P("dp", "ctx", None),
            P("dp", "ctx", None),
            P("dp", "ctx", None),
            P(),
            P("ctx", None),
            P("dp", "ctx", None),
        ),
        out_specs=(
            P("dp", "ctx", None),
            P("dp", "ctx", None),
            P("dp", "ctx", None),
            P("dp", "ctx", None),
            P("ctx", None),
        ),
        check_vma=False,
    )
```

profile of v0, /device:TPU:1, one launch (start us, length us, event | category | flops | bytes accessed | tf_op | source)
XLA Modules:
  0.0 674.6 jit_solution(1039800989723553245)
XLA Ops:
  12.7 2.1 fusion.6
  17.4 183.0 %all-gather.8.cloned.1.call-done = f32[512,128,128]{2,1,0:T(8,128)} async-done(((f32[16,128,128]{2,1,0:T(8,128)}), f32[512,128,128]{2,1,0:T(8,128)}) %all-gather.8.cloned.1.call-update) | async-done | bytes 33554448 | tf_op jit(solution)/shard_map/all_gather | solution.py:14
  200.4 52.2 %while.30 = (s32[]{:T(128)}, f32[16,128,128]{2,1,0:T(8,128)S(1)}, s32[]{:T(128)}, f32[32,16,128,128]{3,2,1,0:T(8,128)}, s32[]{:T(128)}, /*index=5*/s32[]{:T(128)}) while((s32[]{:T(128)}, f32[16,128,128]{2,1,0:T(8,128)S(1)}, s32[]{:T(128)}, f32[32,16,128,128]{3,2,1,0:T(8,128)}, s32[]{:T(128)}, /*index=5*/s32[]{:T(128)}) %tuple.93), condition=%wide.region_1.2_spmd.clone, body=%wide.region_0.1_spmd.clone.sunk | while | flops 786436 | bytes 3145821 | solution.py:22
  213.4 1.7 add_select_fusion.4
  246.1 1.6 add_select_fusion.4
  255.3 19.7 %all-gather.6.cloned.1.call-done = bf16[2048,2048]{1,0:T(8,128)(2,1)} async-done(((bf16[64,2048]{1,0:T(8,128)(2,1)}), bf16[2048,2048]{1,0:T(8,128)(2,1)}) %all-gather.6.cloned.1.call-update) | async-done | bytes 8388624 | tf_op jit(solution)/shard_map/all_gather | solution.py:58
  275.0 5.7 multiply_reduce_fusion
  281.9 5.6 convolution_convert_fusion
  287.6 124.8 %reduce-scatter.2.cloned.1.call-done = bf16[64,2048]{1,0:T(8,128)(2,1)} async-done(((bf16[2048,2048]{1,0:T(8,128)(2,1)}), bf16[64,2048]{1,0:T(8,128)(2,1)}) %reduce-scatter.2.cloned.1.call-update) | async-done | bytes 262160 | tf_op jit(solution)/shard_map/reduce_scatter | solution.py:139
  414.0 1.7 fusion.4
  415.7 1.7 fusion.27
  417.5 2.7 convolution_add_fusion.2
  421.7 2.5 fusion.29
  424.1 2.3 fusion.28
  426.5 2.1 fusion.10
  428.6 5.5 fusion
  434.0 65.0 %all-reduce.2.cloned.1.call-done = bf16[64,2048]{1,0:T(8,128)(2,1)} async-done(((bf16[64,2048]{1,0:T(8,128)(2,1)}), bf16[64,2048]{1,0:T(8,128)(2,1)}) %all-reduce.2.cloned.1.call-update) | async-done | bytes 262160 | tf_op jit(solution)/shard_map/psum | solution.py:147
  499.0 1.8 convert_multiply_fusion
  500.8 103.3 %all-gather.10.cloned.1.call-done = bf16[512,128,128]{2,1,0:T(8,128)(2,1)} async-done(((bf16[16,128,128]{2,1,0:T(8,128)(2,1)}), bf16[512,128,128]{2,1,0:T(8,128)(2,1)}) %all-gather.10.cloned.1.call-update) | async-done | bytes 16777232 | tf_op jit(solution)/shard_map/all_gather | solution.py:27
  604.1 52.7 %while.31 = (s32[]{:T(128)}, f32[16,128,128]{2,1,0:T(8,128)S(1)}, s32[]{:T(128)}, bf16[32,16,128,128]{3,2,1,0:T(8,128)(2,1)}, s32[]{:T(128)}, /*index=5*/s32[]{:T(128)}, s32[]{:T(128)}, s32[]{:T(128)}) while((s32[]{:T(128)}, f32[16,128,128]{2,1,0:T(8,128)S(1)}, s32[]{:T(128)}, bf16[32,16,128,128]{3,2,1,0:T(8,128)(2,1)}, s32[]{:T(128)}, ...), condition=%wide.region_5.6_spmd.clone, body=%wide.region_4.5_spmd.clone.sunk | while | flops 1048584 | bytes 2621595 | solution.py:36
  604.1 1.7 add_select_fusion.5
  656.8 3.1 fusion.2
  659.9 2.0 copy.50
  662.0 3.4 convolution_add_fusion.1
  (117 shorter events, 115.8 us)
Async XLA Ops:
  7.2 267.8 %copy-start = (bf16[1,128,2048]{2,1,0:T(8,128)(2,1)S(1)}, bf16[1,128,2048]{2,1,0:T(8,128)(2,1)}, u32[]{:S(2)}) copy-start(bf16[1,128,2048]{2,1,0:T(8,128)(2,1)} %param.15) | copy-start | bytes 1572868
  7.2 193.3 %all-gather.8.cloned.1.call-start = ((), (), s32[]{:S(2)}) async-start(), calls=%async_computation.4 | async-start | bytes 34603008 | tf_op jit(solution)/shard_map/all_gather | solution.py:14
  8.7 191.7 %copy-start.8 = (bf16[16,8,16,128]{3,2,1,0:T(8,128)(2,1)}, bf16[16,8,16,128]{3,2,1,0:T(8,128)(2,1)S(1)}, u32[]{:S(2)}) copy-start(bf16[16,8,16,128]{3,2,1,0:T(8,128)(2,1)S(1)} %copy.57) | copy-start | bytes 1572868
  9.2 3.5 copy-start.10
  10.6 243.1 %copy-start.5 = (bf16[16,8,16,128]{3,2,1,0:T(8,128)(2,1)}, bf16[16,8,16,128]{3,2,1,0:T(8,128)(2,1)S(1)}, u32[]{:S(2)}) copy-start(bf16[16,8,16,128]{3,2,1,0:T(8,128)(2,1)S(1)} %copy.58) | copy-start | bytes 1572868
  11.9 263.1 %all-gather.6.cloned.1.call-start = ((), (), s32[]{:S(2)}) async-start(), calls=%async_computation.1 | async-start | bytes 8650752 | tf_op jit(solution)/shard_map/all_gather | solution.py:58
  12.6 399.8 %reduce-scatter.2.cloned.1.call-start = ((), (), s32[]{:S(2)}) async-start(), calls=%async_computation.2 | async-start | bytes 8650752 | tf_op jit(solution)/shard_map/reduce_scatter | solution.py:139
  16.1 236.6 %copy-start.2 = (bf16[1,128,2048]{1,2,0:T(8,128)(2,1)}, bf16[1,128,2048]{1,2,0:T(8,128)(2,1)S(1)}, u32[]{:S(2)}) copy-start(bf16[1,128,2048]{1,2,0:T(8,128)(2,1)S(1)} %copy.56) | copy-start | bytes 1572868
  200.4 74.6 %copy-start.13 = (f32[2048]{0:T(1024)S(1)}, f32[2048]{0:T(1024)}, u32[]{:S(2)}) copy-start(f32[2048]{0:T(1024)} %param.13) | copy-start | bytes 24580
  281.9 130.8 %copy-start.3 = (bf16[1,128,2048]{1,2,0:T(8,128)(2,1)S(1)}, bf16[1,128,2048]{1,2,0:T(8,128)(2,1)}, u32[]{:S(2)}) copy-start(bf16[1,128,2048]{1,2,0:T(8,128)(2,1)} %copy-done.2) | copy-start | bytes 1572868
  281.9 130.8 %copy-start.7 = (bf16[128,16,128]{0,2,1:T(8,128)(2,1)S(1)}, bf16[128,16,128]{0,2,1:T(8,128)(2,1)}, u32[]{:S(2)}) copy-start(bf16[128,16,128]{0,2,1:T(8,128)(2,1)} %get-tuple-element.254) | copy-start | bytes 1572868
  287.5 136.6 %copy-start.4 = (bf16[1,128,2048]{1,2,0:T(8,128)(2,1)S(1)}, bf16[1,128,2048]{1,2,0:T(8,128)(2,1)}, u32[]{:S(2)}) copy-start(bf16[1,128,2048]{1,2,0:T(8,128)(2,1)} %copy-done.2) | copy-start | bytes 1572868
  287.6 211.5 %all-reduce.2.cloned.1.call-start = ((), (), s32[]{:S(2)}) async-start(), calls=%async_computation.3 | async-start | bytes 524288 | tf_op jit(solution)/shard_map/psum | solution.py:147
  412.5 191.6 %all-gather.10.cloned.1.call-start = ((), (), s32[]{:S(2)}) async-start(), calls=%async_computation.5 | async-start | bytes 17301504 | tf_op jit(solution)/shard_map/all_gather | solution.py:27
  415.7 4.4 copy-start.12
  434.0 222.8 %copy-start.9 = (bf16[16,8,16,128]{3,2,1,0:T(8,128)(2,1)S(1)}, bf16[16,8,16,128]{3,2,1,0:T(8,128)(2,1)}, u32[]{:S(2)}) copy-start(bf16[16,8,16,128]{3,2,1,0:T(8,128)(2,1)} %copy-done.8) | copy-start | bytes 1572868
  604.1 57.9 %copy-start.6 = (bf16[16,8,16,128]{3,2,1,0:T(8,128)(2,1)S(1)}, bf16[16,8,16,128]{3,2,1,0:T(8,128)(2,1)}, u32[]{:S(2)}) copy-start(bf16[16,8,16,128]{3,2,1,0:T(8,128)(2,1)} %copy-done.5) | copy-start | bytes 1572868
  604.1 62.9 %copy-start.11 = (bf16[1,128,2048]{2,1,0:T(8,128)(2,1)S(1)}, bf16[1,128,2048]{2,1,0:T(8,128)(2,1)}, u32[]{:S(2)}) copy-start(bf16[1,128,2048]{2,1,0:T(8,128)(2,1)} %param.11) | copy-start | bytes 1572868
  656.8 11.2 %copy-start.1 = (bf16[1,128,2048]{2,1,0:T(8,128)(2,1)S(1)}, bf16[1,128,2048]{2,1,0:T(8,128)(2,1)}, u32[]{:S(2)}) copy-start(bf16[1,128,2048]{2,1,0:T(8,128)(2,1)} %param.15) | copy-start | bytes 1572868
Sparse Core Ops, SparseCore 0:
  12.0 188.4 all-gather.7
  202.3 72.6 all-gather.5
  287.7 124.7 reduce-scatter.1
  414.9 84.0 all-reduce.1
  500.9 103.1 all-gather.9
where the time goes:
time: 678 us; the launch traced here: 675 us
  waiting for transfers between devices  497 us (73%)
  other arithmetic  113 us (17%)
  matrix products  40.6 us (6%)
  between operations  14 us (2%)
  local copies, waits for them, and re-layouts  8.44 us (1%)
    all_gather x1, waiting for transfers between devices, carried_in(): everything = lax.all_gather(value, axis)  183 us
    reduce_scatter x1, waiting for transfers between devices, on_device(): lax.psum_scatter(lax.dot_general(normed, upstream, (((0,), (0,)), ((), ()...  125 us
    all_gather x1, waiting for transfers between devices, entering(): everything = lax.all_gather(value.astype(jnp.bfloat16), axis)  103 us
    psum x1, waiting for transfers between devices, on_device(): summed = lax.psum(shares, 'dp').astype(jnp.float32)  65 us
    select_n x32, other arithmetic, entering_turn(): return jnp.where(reached, new, before)  51.8 us
    select_n x32, other arithmetic, carried_turn(): return jnp.where(reached, new, before)  51.4 us
    all_gather x1, waiting for transfers between devices, on_device(): weight = lax.all_gather(out_weight, 'ctx', axis=0, tiled=True)  19.7 us
  transfers between devices with their start and end apart: 5, of which 5 were waited for; matrix products, arithmetic and copies ran while one was open for 12% of the time, Pallas kernels for 0%

commit v1 on v0

--- a/solution.py
+++ b/solution.py
@@ -144,7 +144,7 @@
         scatter_dimension=0,
         tiled=True,
     )
-    summed = lax.psum(shares, "dp").astype(jnp.float32)
+    summed = jnp.sum(lax.all_gather(shares, "dp"), axis=0).astype(jnp.float32)
     grad_weight = summed * loss_scale
     return (mixed[None], grad_queries[None], grad_keys[None], grad_values[None], grad_weight)
 

time: 678 us -> 648 us (0.956)
  waiting for transfers between devices: 497 us -> 465 us
    psum x1 -> x0, waiting for transfers between devices: 65 us -> none  [on_device(): summed = lax.psum(shares, 'dp').astype(jnp.float32)]
    all_gather x0 -> x1, waiting for transfers between devices: none -> 39.4 us  [on_device(): summed = jnp.sum(lax.all_gather(shares, 'dp'), axis=0).astype(jnp.float32)]
  transfers between devices with their start and end apart: 5 -> 5, of which waited for: 5 -> 5; matrix products, arithmetic and copies ran while one was open for 12% -> 13% of each run, Pallas kernels for 0% -> 0%
where the time goes in v1:
time: 648 us; the launch traced here: 644 us
  waiting for transfers between devices  465 us (72%)
  other arithmetic  114 us (18%)
  matrix products  40.6 us (6%)
  between operations  14 us (2%)
  local copies, waits for them, and re-layouts  8.44 us (1%)
    all_gather x1, waiting for transfers between devices, carried_in(): everything = lax.all_gather(value, axis)  183 us
    reduce_scatter x1, waiting for transfers between devices, on_device(): lax.psum_scatter(lax.dot_general(normed, upstream, (((0,), (0,)), ((), ()...  125 us
    all_gather x1, waiting for transfers between devices, entering(): everything = lax.all_gather(value.astype(jnp.bfloat16), axis)  97.4 us
    select_n x32, other arithmetic, entering_turn(): return jnp.where(reached, new, before)  51.8 us
    select_n x32, other arithmetic, carried_turn(): return jnp.where(reached, new, before)  51.4 us
    all_gather x1, waiting for transfers between devices, on_device(): summed = jnp.sum(lax.all_gather(shares, 'dp'), axis=0).astype(jnp.float32)  39.4 us
    all_gather x1, waiting for transfers between devices, on_device(): weight = lax.all_gather(out_weight, 'ctx', axis=0, tiled=True)  19.7 us
  transfers between devices with their start and end apart: 5, of which 5 were waited for; matrix products, arithmetic and copies ran while one was open for 13% of the time, Pallas kernels for 0%

profile of v1, /device:TPU:1, one launch (start us, length us, event | category | flops | bytes accessed | tf_op | source)
XLA Modules:
  0.0 644.1 jit_solution(1740175805880874711)
XLA Ops:
  12.7 2.1 fusion.6
  17.4 183.0 %all-gather.10.cloned.1.call-done = f32[512,128,128]{2,1,0:T(8,128)} async-done(((f32[16,128,128]{2,1,0:T(8,128)}), f32[512,128,128]{2,1,0:T(8,128)}) %all-gather.10.cloned.1.call-update) | async-done | bytes 33554448 | tf_op jit(solution)/shard_map/all_gather | solution.py:14
  200.4 52.2 %while.30 = (s32[]{:T(128)}, f32[16,128,128]{2,1,0:T(8,128)S(1)}, s32[]{:T(128)}, f32[32,16,128,128]{3,2,1,0:T(8,128)}, s32[]{:T(128)}, /*index=5*/s32[]{:T(128)}) while((s32[]{:T(128)}, f32[16,128,128]{2,1,0:T(8,128)S(1)}, s32[]{:T(128)}, f32[32,16,128,128]{3,2,1,0:T(8,128)}, s32[]{:T(128)}, /*index=5*/s32[]{:T(128)}) %tuple.93), condition=%wide.region_1.2_spmd.clone, body=%wide.region_0.1_spmd.clone.sunk | while | flops 786436 | bytes 3145821 | solution.py:22
  213.4 1.7 add_select_fusion.4
  246.1 1.6 add_select_fusion.4
  255.3 19.7 %all-gather.8.cloned.1.call-done = bf16[2048,2048]{1,0:T(8,128)(2,1)} async-done(((bf16[64,2048]{1,0:T(8,128)(2,1)}), bf16[2048,2048]{1,0:T(8,128)(2,1)}) %all-gather.8.cloned.1.call-update) | async-done | bytes 8388624 | tf_op jit(solution)/shard_map/all_gather | solution.py:58
  275.0 5.7 multiply_reduce_fusion
  281.9 5.6 convolution_convert_fusion
  287.6 124.8 %reduce-scatter.2.cloned.1.call-done = bf16[64,2048]{1,0:T(8,128)(2,1)} async-done(((bf16[2048,2048]{1,0:T(8,128)(2,1)}), bf16[64,2048]{1,0:T(8,128)(2,1)}) %reduce-scatter.2.cloned.1.call-update) | async-done | bytes 262160 | tf_op jit(solution)/shard_map/reduce_scatter | solution.py:139
  414.0 1.7 fusion.4
  415.7 1.7 fusion.27
  417.5 2.7 convolution_add_fusion.2
  421.7 2.5 fusion.29
  424.2 2.3 fusion.28
  426.5 2.1 fusion.10
  428.6 5.5 fusion
  434.1 39.4 %all-gather.14.cloned.1.call-done = bf16[512,2048]{1,0:T(8,128)(2,1)} async-done(((bf16[64,2048]{1,0:T(8,128)(2,1)}), bf16[512,2048]{1,0:T(8,128)(2,1)}) %all-gather.14.cloned.1.call-update) | async-done | bytes 2097168 | tf_op jit(solution)/shard_map/all_gather | solution.py:147
  473.4 2.0 reduce_sum.32
  476.2 97.4 %all-gather.12.cloned.1.call-done = bf16[512,128,128]{2,1,0:T(8,128)(2,1)} async-done(((bf16[16,128,128]{2,1,0:T(8,128)(2,1)}), bf16[512,128,128]{2,1,0:T(8,128)(2,1)}) %all-gather.12.cloned.1.call-update) | async-done | bytes 16777232 | tf_op jit(solution)/shard_map/all_gather | solution.py:27
  573.7 52.7 %while.31 = (s32[]{:T(128)}, f32[16,128,128]{2,1,0:T(8,128)S(1)}, s32[]{:T(128)}, bf16[32,16,128,128]{3,2,1,0:T(8,128)(2,1)}, s32[]{:T(128)}, /*index=5*/s32[]{:T(128)}, s32[]{:T(128)}, s32[]{:T(128)}) while((s32[]{:T(128)}, f32[16,128,128]{2,1,0:T(8,128)S(1)}, s32[]{:T(128)}, bf16[32,16,128,128]{3,2,1,0:T(8,128)(2,1)}, s32[]{:T(128)}, ...), condition=%wide.region_5.6_spmd.clone, body=%wide.region_4.5_spmd.clone.sunk | while | flops 1048584 | bytes 2621595 | solution.py:36
  573.7 1.7 add_select_fusion.5
  626.4 3.1 fusion.2
  629.5 2.0 copy.50
  631.5 3.4 convolution_add_fusion.1
  (118 shorter events, 116.6 us)
Async XLA Ops:
  7.2 267.8 %copy-start = (bf16[1,128,2048]{2,1,0:T(8,128)(2,1)S(1)}, bf16[1,128,2048]{2,1,0:T(8,128)(2,1)}, u32[]{:S(2)}) copy-start(bf16[1,128,2048]{2,1,0:T(8,128)(2,1)} %param.15) | copy-start | bytes 1572868
  7.2 193.3 %all-gather.10.cloned.1.call-start = ((), (), s32[]{:S(2)}) async-start(), calls=%async_computation.3 | async-start | bytes 34603008 | tf_op jit(solution)/shard_map/all_gather | solution.py:14
  8.7 191.7 %copy-start.8 = (bf16[16,8,16,128]{3,2,1,0:T(8,128)(2,1)}, bf16[16,8,16,128]{3,2,1,0:T(8,128)(2,1)S(1)}, u32[]{:S(2)}) copy-start(bf16[16,8,16,128]{3,2,1,0:T(8,128)(2,1)S(1)} %copy.57) | copy-start | bytes 1572868
  9.2 3.5 copy-start.10
  10.6 243.1 %copy-start.5 = (bf16[16,8,16,128]{3,2,1,0:T(8,128)(2,1)}, bf16[16,8,16,128]{3,2,1,0:T(8,128)(2,1)S(1)}, u32[]{:S(2)}) copy-start(bf16[16,8,16,128]{3,2,1,0:T(8,128)(2,1)S(1)} %copy.58) | copy-start | bytes 1572868
  11.9 263.1 %all-gather.8.cloned.1.call-start = ((), (), s32[]{:S(2)}) async-start(), calls=%async_computation.1 | async-start | bytes 8650752 | tf_op jit(solution)/shard_map/all_gather | solution.py:58
  12.6 399.8 %reduce-scatter.2.cloned.1.call-start = ((), (), s32[]{:S(2)}) async-start(), calls=%async_computation.2 | async-start | bytes 8650752 | tf_op jit(solution)/shard_map/reduce_scatter | solution.py:139
  16.1 236.6 %copy-start.2 = (bf16[1,128,2048]{1,2,0:T(8,128)(2,1)}, bf16[1,128,2048]{1,2,0:T(8,128)(2,1)S(1)}, u32[]{:S(2)}) copy-start(bf16[1,128,2048]{1,2,0:T(8,128)(2,1)S(1)} %copy.56) | copy-start | bytes 1572868
  200.4 74.6 %copy-start.13 = (f32[2048]{0:T(1024)S(1)}, f32[2048]{0:T(1024)}, u32[]{:S(2)}) copy-start(f32[2048]{0:T(1024)} %param.13) | copy-start | bytes 24580
  281.9 130.8 %copy-start.3 = (bf16[1,128,2048]{1,2,0:T(8,128)(2,1)S(1)}, bf16[1,128,2048]{1,2,0:T(8,128)(2,1)}, u32[]{:S(2)}) copy-start(bf16[1,128,2048]{1,2,0:T(8,128)(2,1)} %copy-done.2) | copy-start | bytes 1572868
  281.9 130.8 %copy-start.7 = (bf16[128,16,128]{0,2,1:T(8,128)(2,1)S(1)}, bf16[128,16,128]{0,2,1:T(8,128)(2,1)}, u32[]{:S(2)}) copy-start(bf16[128,16,128]{0,2,1:T(8,128)(2,1)} %get-tuple-element.254) | copy-start | bytes 1572868
  287.5 136.6 %copy-start.4 = (bf16[1,128,2048]{1,2,0:T(8,128)(2,1)S(1)}, bf16[1,128,2048]{1,2,0:T(8,128)(2,1)}, u32[]{:S(2)}) copy-start(bf16[1,128,2048]{1,2,0:T(8,128)(2,1)} %copy-done.2) | copy-start | bytes 1572868
  287.6 185.9 %all-gather.14.cloned.1.call-start = ((), (), s32[]{:S(2)}) async-start(), calls=%async_computation.5 | async-start | bytes 2359296 | tf_op jit(solution)/shard_map/all_gather | solution.py:147
  412.5 161.2 %all-gather.12.cloned.1.call-start = ((), (), s32[]{:S(2)}) async-start(), calls=%async_computation.4 | async-start | bytes 17301504 | tf_op jit(solution)/shard_map/all_gather | solution.py:27
  415.7 4.4 copy-start.12
  434.1 192.3 %copy-start.9 = (bf16[16,8,16,128]{3,2,1,0:T(8,128)(2,1)S(1)}, bf16[16,8,16,128]{3,2,1,0:T(8,128)(2,1)}, u32[]{:S(2)}) copy-start(bf16[16,8,16,128]{3,2,1,0:T(8,128)(2,1)} %copy-done.8) | copy-start | bytes 1572868
  573.6 57.9 %copy-start.6 = (bf16[16,8,16,128]{3,2,1,0:T(8,128)(2,1)S(1)}, bf16[16,8,16,128]{3,2,1,0:T(8,128)(2,1)}, u32[]{:S(2)}) copy-start(bf16[16,8,16,128]{3,2,1,0:T(8,128)(2,1)} %copy-done.5) | copy-start | bytes 1572868
  573.6 62.9 %copy-start.11 = (bf16[1,128,2048]{2,1,0:T(8,128)(2,1)S(1)}, bf16[1,128,2048]{2,1,0:T(8,128)(2,1)}, u32[]{:S(2)}) copy-start(bf16[1,128,2048]{2,1,0:T(8,128)(2,1)} %param.11) | copy-start | bytes 1572868
  626.4 11.2 %copy-start.1 = (bf16[1,128,2048]{2,1,0:T(8,128)(2,1)S(1)}, bf16[1,128,2048]{2,1,0:T(8,128)(2,1)}, u32[]{:S(2)}) copy-start(bf16[1,128,2048]{2,1,0:T(8,128)(2,1)} %param.15) | copy-start | bytes 1572868
Sparse Core Ops, SparseCore 0:
  12.0 188.4 all-gather.9
  202.3 72.6 all-gather.7
  287.7 124.7 reduce-scatter.1
  414.9 58.4 all-gather.13
  475.1 98.4 all-gather.11
